TPU v7x, 128 devices: a whole 4x4x4 slice. The times are simulated.
128 devices in a mesh: wide: 32 (over z, y, core), narrow: 4 (over x).
Axes of the slice: x: 4, y: 4, z: 4, core: 2. Of those that a mesh axis runs over, the one named last changes fastest.
Arguments:
- frames: float32 [131072, 440], P(('wide', 'narrow')), may hold values from -8 to 8
- targets: float32 [131072, 2048], P(('wide', 'narrow')), may hold values from -7 to 7
- projection: float32 [128, 440, 512], P(('wide', 'narrow')), may hold values from -0.25 to 0.25
- phases: float32 [128, 512], P(('wide', 'narrow')), may hold values from 0 to 6.283185
- block_order: int32 [128], replicated, may hold values from 0 to 127, each once
Outputs:
- residual: float32 [131072, 2048], P(('wide', 'narrow'))
- weights: float32 [2, 512, 2048], replicated
Inputs may be any that keep to these rules, and one draw needn't show every extreme that they name: `block_order`: a permutation; steps use its first 2 entries.
All inputs are finite; a program needn't handle non-finite values.
Results may differ from a plain program's by a relative error of at most 0.0003.
Values sent between devices are 32-bit elements; how exact they have to be, the bound alone decides.
A program may use at most 128 MiB of HBM per device.

v0:
```python
import jax
import jax.numpy as jnp
from jax import lax
from jax.sharding import PartitionSpec as P

STEPS = 2


def from_root(value, axis, source):
    kept = jnp.where(lax.axis_index(axis) == source, value, 0).astype(value.dtype)
    return lax.psum(kept, axis)


def features_of(frames, block_proj, block_phase):
    inner = jnp.dot(
        frames, block_proj, precision=lax.Precision.HIGHEST, preferred_element_type=jnp.float32
    )
    return jnp.sqrt(2.0 / block_proj.shape[1]) * jnp.cos(inner + block_phase[None, :])


def local_product(left, right):
    return jnp.dot(
        left.T, right, precision=lax.Precision.HIGHEST, preferred_element_type=jnp.float32
    )


def solve_block(gram_sum, cross_sum):
    width = gram_sum.shape[0]
    damping = 0.1 * jnp.trace(gram_sum) / width
    factor = jnp.linalg.cholesky(gram_sum + damping * jnp.eye(width, dtype=gram_sum.dtype))
    return jax.scipy.linalg.cho_solve((factor, True), cross_sum)


def per_device(frames, targets, projection, phases, block_order):
    feature_list = []
    for step_index in range(STEPS):
        block_proj, block_phase = (
            from_root(projection, ("wide", "narrow"), block_order[step_index]),
            from_root(phases, ("wide", "narrow"), block_order[step_index]),
        )
        feature_list.append(features_of(frames, block_proj[0], block_phase[0]))
    grams_local = jnp.stack([local_product(feats, feats) for feats in feature_list])
    grams_all = lax.psum(grams_local, ("wide", "narrow"))
    residual = targets
    solved = []
    for step_index in range(STEPS):
        feats = feature_list[step_index]
        cross_local = local_product(feats, residual)
        gram_sum = grams_all[step_index]
        cross_sum = lax.psum(cross_local, ("wide", "narrow"))
        weights = solve_block(gram_sum, cross_sum)
        residual = residual - jnp.dot(
            feats, weights, precision=lax.Precision.HIGHEST, preferred_element_type=jnp.float32
        )
        solved.append(weights)
    return (residual, jnp.stack(solved))


def solution(mesh):
    return jax.shard_map(
        per_device,
        mesh=mesh,
        in_specs=(
            P(("wide", "narrow"), None),
            P(("wide", "narrow"), None),
            P(("wide", "narrow"), None, None),
            P(("wide", "narrow"), None),
            P(),
        ),
        out_specs=(P(("wide", "narrow"), None), P()),
        check_vma=False,
    )
```

profile of v0, /device:TPU:1, one launch (start us, length us, event | category | flops | bytes accessed | tf_op | source)
XLA Modules:
  0.0 860.8 jit_solution(9181122696572727834)
XLA Ops:
  12.6 69.1 %all-reduce.1 = (f32[512]{0:T(512)S(1)}, f32[512]{0:T(512)S(1)}) all-reduce(f32[512]{0:T(512)S(1)} %bitcast.163, f32[512]{0:T(512)S(1)} %bitcast.162), channel_id=1, replica_groups=mesh['wide'=32,'narrow'=4] {'wide','narrow'}, use_global_device_ids=true, to_apply=%region_1.2 | all-reduce | flops 1024 | bytes 8192 | tf_op jit(solution)/shard_map/psum | solution.py:11
  81.7 85.6 %all-reduce.12.cloned.1.call-done = (f32[440,512]{1,0:T(8,128)}, f32[440,512]{1,0:T(8,128)}) async-done(((f32[440,512]{1,0:T(8,128)}, f32[440,512]{1,0:T(8,128)}), (f32[440,512]{1,0:T(8,128)}, f32[440,512]{1,0:T(8,128)})) %all-reduce.12.cloned.1.call-update) | async-done | bytes 1802256 | tf_op jit(solution)/shard_map/psum | solution.py:11
  167.3 11.2 %cosine_multiply_fusion.1 = f32[512,1024]{1,0:T(8,128)S(1)} fusion(f32[440,512]{1,0:T(8,128)} %get-tuple-element.42, f32[1024,440]{0,1:T(8,128)S(1)} %copy-done, f32[512]{0:T(512)S(1)} %get-tuple-element.38), kind=kOutput, calls=%fused_computation.61 | convolution fusion | flops 2769289216 | bytes 4802560 | tf_op jit(solution)/shard_map/dot_general | solution.py:15
  182.4 10.3 %cosine_multiply_fusion = f32[512,1024]{1,0:T(8,128)S(1)} fusion(f32[440,512]{1,0:T(8,128)S(1)} %copy-done.17, f32[1024,440]{0,1:T(8,128)S(1)} %copy-done, f32[512]{0:T(512)S(1)} %get-tuple-element.39), kind=kOutput, calls=%fused_computation.60 | convolution fusion | flops 2769289216 | bytes 4802560 | tf_op jit(solution)/shard_map/dot_general | solution.py:15
  197.7 15.2 %fusion.117 = f32[512,2048]{1,0:T(8,128)} fusion(f32[512,1024]{1,0:T(8,128)S(1)} %cosine_multiply_fusion.1, f32[1024,2048]{1,0:T(8,128)S(1)} %bitcast.159), kind=kOutput, calls=%fused_computation.198 | convolution fusion | flops 12884901888 | bytes 14680064 | tf_op jit(solution)/shard_map/dot_general | solution.py:22
  214.9 156.2 %all-reduce.10.cloned.1.call-done = (f32[512,2048]{1,0:T(8,128)}, f32[2,512,512]{1,2,0:T(8,128)}) async-done(((f32[512,2048]{1,0:T(8,128)}, f32[2,512,512]{1,2,0:T(8,128)}), (f32[512,2048]{1,0:T(8,128)}, f32[2,512,512]{1,2,0:T(8,128)})) %all-reduce.10.cloned.1.call-update) | async-done | bytes 6291472 | tf_op jit(solution)/shard_map/psum | solution.py:50
  381.9 11.7 %cholesky.358 = f32[128,128]{1,0:T(8,128)S(1)} custom-call(f32[128,128]{1,0:T(8,128)S(1)} %cholesky.439), custom_call_target="Cholesky" | custom-call | tf_op jit(solution)/shard_map/jit(cholesky)/cholesky | solution.py:30
  394.4 11.7 %cholesky.286 = f32[128,128]{1,0:T(8,128)S(1)} custom-call(f32[128,128]{1,0:T(8,128)S(1)} %cholesky.426), custom_call_target="Cholesky" | custom-call | tf_op jit(solution)/shard_map/jit(cholesky)/cholesky | solution.py:30
  417.4 10.0 %custom-call.33 = f32[1,128,128]{1,2,0:T(8,128)S(1)} custom-call(f32[1,128,128]{2,1,0:T(8,128)S(1)} %get-tuple-element.61), custom_call_target="InvertDiagBlocksLowerTriangular" | custom-call | tf_op jit(solution)/shard_map/jit(cholesky)/cholesky | solution.py:30
  430.0 11.7 %cholesky.377 = f32[128,128]{1,0:T(8,128)S(1)} custom-call(f32[128,128]{1,0:T(8,128)S(1)} %cholesky.443), custom_call_target="Cholesky" | custom-call | tf_op jit(solution)/shard_map/jit(cholesky)/cholesky | solution.py:30
  453.8 11.9 %cholesky.398 = f32[128,128]{1,0:T(8,128)S(1)} custom-call(f32[128,128]{1,0:T(8,128)S(1)} %cholesky.448), custom_call_target="Cholesky" | custom-call | tf_op jit(solution)/shard_map/jit(cholesky)/cholesky | solution.py:30
  465.7 9.8 %custom-call.35 = f32[1,128,128]{1,2,0:T(8,128)S(1)} custom-call(f32[1,128,128]{2,1,0:T(8,128)S(1)} %get-tuple-element.55), custom_call_target="InvertDiagBlocksLowerTriangular" | custom-call | tf_op jit(solution)/shard_map/jit(cholesky)/cholesky | solution.py:30
  477.0 11.7 %cholesky.415 = f32[128,128]{1,0:T(8,128)S(1)} custom-call(f32[128,128]{1,0:T(8,128)S(1)} %convolution_subtract_fusion.14), custom_call_target="Cholesky" | custom-call | tf_op jit(solution)/shard_map/jit(cholesky)/cholesky | solution.py:30
  489.6 11.7 %cholesky.305 = f32[128,128]{1,0:T(8,128)S(1)} custom-call(f32[128,128]{1,0:T(8,128)S(1)} %cholesky.430), custom_call_target="Cholesky" | custom-call | tf_op jit(solution)/shard_map/jit(cholesky)/cholesky | solution.py:30
  501.9 10.2 %custom-call.30 = f32[1,128,128]{1,2,0:T(8,128)S(1)} custom-call(f32[1,128,128]{2,1,0:T(8,128)S(1)} %get-tuple-element.68), custom_call_target="InvertDiagBlocksLowerTriangular" | custom-call | tf_op jit(solution)/shard_map/jit(cholesky)/cholesky | solution.py:30
  512.9 11.7 %cholesky.326 = f32[128,128]{1,0:T(8,128)S(1)} custom-call(f32[128,128]{1,0:T(8,128)S(1)} %cholesky.435), custom_call_target="Cholesky" | custom-call | tf_op jit(solution)/shard_map/jit(cholesky)/cholesky | solution.py:30
  535.7 11.9 %cholesky.343 = f32[128,128]{1,0:T(8,128)S(1)} custom-call(f32[128,128]{1,0:T(8,128)S(1)} %convolution_subtract_fusion.15), custom_call_target="Cholesky" | custom-call | tf_op jit(solution)/shard_map/jit(cholesky)/cholesky | solution.py:30
  559.4 39.3 %custom-call.32 = f32[4,128,128]{1,2,0:T(8,128)S(1)} custom-call(f32[4,128,128]{2,1,0:T(8,128)S(1)} %get-tuple-element.18), custom_call_target="InvertDiagBlocksLowerTriangular" | custom-call | tf_op jit(solution)/shard_map/jit(_cho_solve)/triangular_solve | solution.py:31
  623.3 16.1 %convolution_subtract_fusion.1 = f32[1024,2048]{1,0:T(8,128)S(1)} fusion(f32[1024,2048]{1,0:T(8,128)S(1)} %bitcast.161, f32[512,1024]{1,0:T(8,128)S(1)} %copy-done.6, f32[128,2048]{1,0:T(8,128)S(1)} %fusion.95, f32[128,2048]{1,0:T(8,128)} %copy-done.7, f32[128,2048]{1,0:T(8,128)} %copy-done.9, f32[128,2048]{1,0:T(8,128)} %fusion.90), kind=kOutput, calls=%fused_computation.8 | convolution fusion | flops 12890144768 | bytes 23068672 | tf_op jit(solution)/shard_map/dot_general | solution.py:52
  642.8 15.6 %fusion.118 = f32[512,2048]{1,0:T(8,128)} fusion(f32[512,1024]{1,0:T(8,128)S(1)} %copy-done.4, f32[1024,2048]{1,0:T(8,128)S(1)} %convolution_subtract_fusion.1), kind=kOutput, calls=%fused_computation.199 | convolution fusion | flops 12884901888 | bytes 14680064 | tf_op jit(solution)/shard_map/dot_general | solution.py:22
  664.6 11.9 %while.5 = (s32[]{:T(128)}, f32[512,512]{1,0:T(8,128)}, s32[4,2]{0,1:T(2,128)S(1)}, f32[4,128,128]{2,1,0:T(8,128)S(1)}, s32[]{:T(128)}) while((s32[]{:T(128)}, f32[512,512]{1,0:T(8,128)}, s32[4,2]{0,1:T(2,128)S(1)}, f32[4,128,128]{2,1,0:T(8,128)S(1)}, s32[]{:T(128)}) %tuple.74), condition=%wide.while_cond.clone, body=%wide.while_body.clone.sunk | while | flops 2 | bytes 131189 | solution.py:31
  677.2 40.3 %custom-call.36 = f32[4,128,128]{1,2,0:T(8,128)S(1)} custom-call(f32[4,128,128]{2,1,0:T(8,128)} %copy-done.18), custom_call_target="InvertDiagBlocksLowerTriangular" | custom-call | tf_op jit(solution)/shard_map/jit(_cho_solve)/triangular_solve | solution.py:31
  721.7 89.9 %all-reduce.8.cloned.1.call-done = f32[512,2048]{1,0:T(8,128)} async-done(((f32[512,2048]{1,0:T(8,128)}), f32[512,2048]{1,0:T(8,128)}) %all-reduce.8.cloned.1.call-update) | async-done | bytes 4194320 | tf_op jit(solution)/shard_map/psum | solution.py:50
  831.7 16.0 %convolution_subtract_fusion = f32[1024,2048]{1,0:T(8,128)} fusion(f32[1024,2048]{1,0:T(8,128)S(1)} %bitcast.157, f32[512,1024]{1,0:T(8,128)S(1)} %copy-done.4, f32[128,2048]{1,0:T(8,128)S(1)} %fusion.102, f32[128,2048]{1,0:T(8,128)S(1)} %fusion.100, f32[128,2048]{1,0:T(8,128)S(1)} %fusion.98, f32[128,2048]{1,0:T(8,128)S(1)} %fusion.97), kind=kOutput, calls=%fused_computation.7 | convolution fusion | flops 12890144768 | bytes 23068672 | tf_op jit(solution)/shard_map/dot_general | solution.py:52
  (173 shorter events, 157.3 us)
Async XLA Ops:
  7.2 160.2 %copy-start = (f32[1024,440]{0,1:T(8,128)S(1)}, f32[1024,440]{0,1:T(8,128)}, u32[]{:S(2)}) copy-start(f32[1024,440]{0,1:T(8,128)} %param.8) | copy-start | bytes 5406724
  7.2 5.4 copy-start.19
  7.2 160.1 %all-reduce.12.cloned.1.call-start = ((), (), s32[]{:S(2)}) async-start(), calls=%async_computation.2 | async-start | bytes 3604480 | tf_op jit(solution)/shard_map/psum | solution.py:11
  12.6 358.6 %all-reduce.10.cloned.1.call-start = ((), (), s32[]{:S(2)}) async-start(), calls=%async_computation.1 | async-start | bytes 12582912 | tf_op jit(solution)/shard_map/psum | solution.py:50
  178.6 19.1 %copy-start.5 = (f32[512,1024]{1,0:T(8,128)}, f32[512,1024]{1,0:T(8,128)S(1)}, u32[]{:S(2)}) copy-start(f32[512,1024]{1,0:T(8,128)S(1)} %cosine_multiply_fusion.1) | copy-start | bytes 6291460
  178.6 3.8 copy-start.17
  178.6 19.0 %slice-start.2 = ((s8[8388608]{0:T(1024)(128)(4,1)}), s8[4194304]{0:T(1024)(128)(4,1)S(1)}, s32[]{:S(2)}) async-start(s8[8388608]{0:T(1024)(128)(4,1)} %bitcast.158), calls=%async_computation.5 | async-start | bytes 8388608
  182.4 15.3 %slice-start.3 = ((s8[8388608]{0:T(1024)(128)(4,1)}), s8[4194304]{0:T(1024)(128)(4,1)S(1)}, s32[]{:S(2)}) async-start(s8[8388608]{0:T(1024)(128)(4,1)} %bitcast.158), calls=%async_computation.6 | async-start | bytes 8388608
  214.4 597.3 %all-reduce.8.cloned.1.call-start = ((), (), s32[]{:S(2)}) async-start(), calls=%async_computation | async-start | bytes 8388608 | tf_op jit(solution)/shard_map/psum | solution.py:50
  381.9 107.0 %copy-start.15 = (f32[512,512]{1,0:T(8,128)S(1)}, f32[512,512]{1,0:T(8,128)}, u32[]{:S(2)}) copy-start(f32[512,512]{1,0:T(8,128)} %get-tuple-element.81) | copy-start | bytes 3145732
  488.7 62.2 %copy-start.10 = (f32[512,512]{1,0:T(8,128)}, f32[512,512]{1,0:T(8,128)S(1)}, u32[]{:S(2)}) copy-start(f32[512,512]{1,0:T(8,128)S(1)} %get-tuple-element.53) | copy-start | bytes 3145732
  559.4 47.4 %copy-start.12 = (f32[512,512]{1,0:T(8,128)}, f32[512,512]{1,0:T(8,128)S(1)}, u32[]{:S(2)}) copy-start(f32[512,512]{1,0:T(8,128)S(1)} %get-tuple-element.187) | copy-start | bytes 3145732
  601.0 3.5 copy-start.13
  610.9 12.3 %slice-start.4 = ((s8[8388608]{0:T(1024)(128)(4,1)}), s8[4194304]{0:T(1024)(128)(4,1)S(1)}, s32[]{:S(2)}) async-start(s8[8388608]{0:T(1024)(128)(4,1)} %bitcast.160), calls=%async_computation.7 | async-start | bytes 8388608
  614.0 7.2 copy-start.7
  616.6 6.7 slice-start.5
  617.6 3.7 copy-start.9
  617.7 5.6 copy-start.6
  623.3 19.5 %copy-start.4 = (f32[512,1024]{1,0:T(8,128)S(1)}, f32[512,1024]{1,0:T(8,128)}, u32[]{:S(2)}) copy-start(f32[512,1024]{1,0:T(8,128)} %copy-done.3) | copy-start | bytes 6291460
  813.9 3.5 copy-start.11
  814.0 3.5 copy-start.14
  825.0 6.7 slice-start
  827.5 4.1 slice-start.1
  849.9 4.0 copy-start.1
  (5 other events, 8.6 us)
Sparse Core Ops, SparseCore 0:
  13.6 153.6 all-reduce.11
  214.5 156.5 all-reduce.9
  658.6 153.0 all-reduce.7
where the time goes:
time: 871 us; the launch traced here: 861 us
  waiting for transfers between devices  332 us (38%)
  other arithmetic  261 us (30%)
  matrix products  143 us (16%)
  blocking collectives  69.1 us (8%)
  local copies, waits for them, and re-layouts  32.4 us (4%)
  between operations  22.6 us (3%)
    psum x2, waiting for transfers between devices, per_device(): cross_sum = lax.psum(cross_local, ('wide', 'narrow'))  246 us
    another operation x30, other arithmetic, solve_block(): jnp.linalg.cholesky(gram_sum + damping * jnp.eye(width, dtype=gram_sum.dt...  159 us
    psum x1, waiting for transfers between devices, from_root(): return lax.psum(kept, axis)  85.6 us
    another operation x5, other arithmetic, solve_block(): return jax.scipy.linalg.cho_solve((factor, True), cross_sum)  82.1 us
    psum x1, blocking collectives, from_root(): return lax.psum(kept, axis)  69.1 us
    another operation x28, matrix products, solve_block(): return jax.scipy.linalg.cho_solve((factor, True), cross_sum)  44.2 us
    dot_general x4, matrix products, local_product(): jnp.dot(left.T, right, precision=lax.Precision.HIGHEST, preferred_element...  38.1 us
    dot_general x2, matrix products, per_device(): jnp.dot(feats, weights, precision=lax.Precision.HIGHEST, preferred_elemen...  32.2 us
  transfers between devices with their start and end apart: 3, of which 3 were waited for; matrix products, arithmetic and copies ran while one was open for 7% of the time, Pallas kernels for 0%

commit v1 on v0

--- a/solution.py
+++ b/solution.py
@@ -47,7 +47,9 @@
         feats = feature_list[step_index]
         cross_local = local_product(feats, residual)
         gram_sum = grams_all[step_index]
-        cross_sum = lax.psum(cross_local, ("wide", "narrow"))
+        cross_sum = cross_local
+        for name in ("wide", "narrow"):
+            cross_sum = lax.psum(cross_sum, name)
         weights = solve_block(gram_sum, cross_sum)
         residual = residual - jnp.dot(
             feats, weights, precision=lax.Precision.HIGHEST, preferred_element_type=jnp.float32

time: 871 us -> 941 us (1.080)
  waiting for transfers between devices: 332 us -> 394 us
    psum x2 -> x5, waiting for transfers between devices: 246 us -> 308 us  [the longest x4 178 us: per_device(): cross_sum = lax.psum(cross_sum, name)]
  transfers between devices with their start and end apart: 3 -> 6, of which waited for: 3 -> 4; matrix products, arithmetic and copies ran while one was open for 7% -> 33% of each run, Pallas kernels for 0% -> 0%
where the time goes in v1:
time: 941 us; the launch traced here: 931 us
  waiting for transfers between devices  394 us (42%)
  other arithmetic  263 us (28%)
  matrix products  148 us (16%)
  blocking collectives  69.2 us (7%)
  local copies, waits for them, and re-layouts  33.6 us (4%)
  between operations  22.8 us (2%)
    psum x4, waiting for transfers between devices, per_device(): cross_sum = lax.psum(cross_sum, name)  178 us
    another operation x30, other arithmetic, solve_block(): jnp.linalg.cholesky(gram_sum + damping * jnp.eye(width, dtype=gram_sum.dt...  160 us
    psum x1, waiting for transfers between devices, per_device(): grams_all = lax.psum(grams_local, ('wide', 'narrow'))  131 us
    psum x1, waiting for transfers between devices, from_root(): return lax.psum(kept, axis)  85.5 us
    another operation x5, other arithmetic, solve_block(): return jax.scipy.linalg.cho_solve((factor, True), cross_sum)  82.8 us
    psum x1, blocking collectives, from_root(): return lax.psum(kept, axis)  69.2 us
    another operation x28, matrix products, solve_block(): return jax.scipy.linalg.cho_solve((factor, True), cross_sum)  44.1 us
    dot_general x4, matrix products, local_product(): jnp.dot(left.T, right, precision=lax.Precision.HIGHEST, preferred_element...  39.8 us
  transfers between devices with their start and end apart: 6, of which 4 were waited for; matrix products, arithmetic and copies ran while one was open for 33% of the time, Pallas kernels for 0%

profile of v1, /device:TPU:1, one launch (start us, length us, event | category | flops | bytes accessed | tf_op | source)
XLA Modules:
  0.0 930.6 jit_solution(10149474691988061991)
XLA Ops:
  12.6 69.2 %all-reduce.1 = (f32[512]{0:T(512)S(1)}, f32[512]{0:T(512)S(1)}) all-reduce(f32[512]{0:T(512)S(1)} %bitcast.161, f32[512]{0:T(512)S(1)} %bitcast.160), channel_id=1, replica_groups=mesh['wide'=32,'narrow'=4] {'wide','narrow'}, use_global_device_ids=true, to_apply=%region_1.2 | all-reduce | flops 1024 | bytes 8192 | tf_op jit(solution)/shard_map/psum | solution.py:11
  81.8 85.5 %all-reduce.20.cloned.1.call-done = (f32[440,512]{1,0:T(8,128)}, f32[440,512]{1,0:T(8,128)}) async-done(((f32[440,512]{1,0:T(8,128)}, f32[440,512]{1,0:T(8,128)}), (f32[440,512]{1,0:T(8,128)}, f32[440,512]{1,0:T(8,128)})) %all-reduce.20.cloned.1.call-update) | async-done | bytes 1802256 | tf_op jit(solution)/shard_map/psum | solution.py:11
  167.3 11.2 %cosine_multiply_fusion.1 = f32[512,1024]{1,0:T(8,128)S(1)} fusion(f32[440,512]{1,0:T(8,128)} %get-tuple-element.40, f32[1024,440]{0,1:T(8,128)S(1)} %copy-done, f32[512]{0:T(512)S(1)} %get-tuple-element.38), kind=kOutput, calls=%fused_computation.61 | convolution fusion | flops 2769289216 | bytes 4802560 | tf_op jit(solution)/shard_map/dot_general | solution.py:15
  182.4 10.5 %cosine_multiply_fusion = f32[512,1024]{1,0:T(8,128)S(1)} fusion(f32[440,512]{1,0:T(8,128)S(1)} %copy-done.17, f32[1024,440]{0,1:T(8,128)S(1)} %copy-done, f32[512]{0:T(512)S(1)} %get-tuple-element.39), kind=kOutput, calls=%fused_computation.60 | convolution fusion | flops 2769289216 | bytes 4802560 | tf_op jit(solution)/shard_map/dot_general | solution.py:15
  200.2 17.3 %fusion.117 = f32[512,2048]{1,0:T(8,128)} fusion(f32[512,1024]{1,0:T(8,128)S(1)} %copy-done.6, f32[1024,2048]{1,0:T(8,128)} %param.9), kind=kOutput, calls=%fused_computation.198 | convolution fusion | flops 12884901888 | bytes 14680064 | tf_op jit(solution)/shard_map/dot_general | solution.py:22
  217.6 130.7 %all-reduce.10.cloned.1.call-done = f32[2,512,512]{1,2,0:T(8,128)} async-done(((f32[2,512,512]{1,2,0:T(8,128)}), f32[2,512,512]{1,2,0:T(8,128)}) %all-reduce.10.cloned.1.call-update) | async-done | bytes 2097168 | tf_op jit(solution)/shard_map/psum | solution.py:43
  358.8 11.7 %cholesky.286 = f32[128,128]{1,0:T(8,128)S(1)} custom-call(f32[128,128]{1,0:T(8,128)S(1)} %cholesky.426), custom_call_target="Cholesky" | custom-call | tf_op jit(solution)/shard_map/jit(cholesky)/cholesky | solution.py:30
  370.6 92.0 %all-reduce.12.cloned.1.call-done = f32[512,2048]{1,0:T(8,128)} async-done(((f32[512,2048]{1,0:T(8,128)}), f32[512,2048]{1,0:T(8,128)}) %all-reduce.12.cloned.1.call-update) | async-done | bytes 4194320 | tf_op jit(solution)/shard_map/psum | solution.py:52
  473.5 11.7 %cholesky.305 = f32[128,128]{1,0:T(8,128)S(1)} custom-call(f32[128,128]{1,0:T(8,128)S(1)} %cholesky.430), custom_call_target="Cholesky" | custom-call | tf_op jit(solution)/shard_map/jit(cholesky)/cholesky | solution.py:30
  495.7 11.9 %cholesky.326 = f32[128,128]{1,0:T(8,128)S(1)} custom-call(f32[128,128]{1,0:T(8,128)S(1)} %cholesky.435), custom_call_target="Cholesky" | custom-call | tf_op jit(solution)/shard_map/jit(cholesky)/cholesky | solution.py:30
  507.6 9.8 %custom-call.31 = f32[1,128,128]{1,2,0:T(8,128)S(1)} custom-call(f32[1,128,128]{2,1,0:T(8,128)S(1)} %get-tuple-element.63), custom_call_target="InvertDiagBlocksLowerTriangular" | custom-call | tf_op jit(solution)/shard_map/jit(cholesky)/cholesky | solution.py:30
  518.1 11.7 %cholesky.343 = f32[128,128]{1,0:T(8,128)S(1)} custom-call(f32[128,128]{1,0:T(8,128)S(1)} %convolution_subtract_fusion.15), custom_call_target="Cholesky" | custom-call | tf_op jit(solution)/shard_map/jit(cholesky)/cholesky | solution.py:30
  543.6 39.8 %custom-call.32 = f32[4,128,128]{1,2,0:T(8,128)S(1)} custom-call(f32[4,128,128]{2,1,0:T(8,128)S(1)} %get-tuple-element.18), custom_call_target="InvertDiagBlocksLowerTriangular" | custom-call | tf_op jit(solution)/shard_map/jit(_cho_solve)/triangular_solve | solution.py:31
  608.0 16.1 %convolution_subtract_fusion.1 = f32[1024,2048]{1,0:T(8,128)S(1)} fusion(f32[1024,2048]{1,0:T(8,128)S(1)} %bitcast.159, f32[512,1024]{1,0:T(8,128)S(1)} %copy-done.7, f32[128,2048]{1,0:T(8,128)S(1)} %fusion.95, f32[128,2048]{1,0:T(8,128)} %copy-done.8, f32[128,2048]{1,0:T(8,128)} %copy-done.10, f32[128,2048]{1,0:T(8,128)} %fusion.90), kind=kOutput, calls=%fused_computation.8 | convolution fusion | flops 12890144768 | bytes 23068672 | tf_op jit(solution)/shard_map/dot_general | solution.py:54
  627.5 15.2 %fusion.118 = f32[512,2048]{1,0:T(8,128)} fusion(f32[512,1024]{1,0:T(8,128)S(1)} %copy-done.4, f32[1024,2048]{1,0:T(8,128)S(1)} %convolution_subtract_fusion.1), kind=kOutput, calls=%fused_computation.199 | convolution fusion | flops 12884901888 | bytes 14680064 | tf_op jit(solution)/shard_map/dot_general | solution.py:22
  644.0 11.7 %cholesky.358 = f32[128,128]{1,0:T(8,128)S(1)} custom-call(f32[128,128]{1,0:T(8,128)S(1)} %cholesky.439), custom_call_target="Cholesky" | custom-call | tf_op jit(solution)/shard_map/jit(cholesky)/cholesky | solution.py:30
  668.7 85.7 %all-reduce.16.cloned.1.call-done = f32[512,2048]{1,0:T(8,128)} async-done(((f32[512,2048]{1,0:T(8,128)}), f32[512,2048]{1,0:T(8,128)}) %all-reduce.16.cloned.1.call-update) | async-done | bytes 4194320 | tf_op jit(solution)/shard_map/psum | solution.py:52
  755.7 11.7 %cholesky.377 = f32[128,128]{1,0:T(8,128)S(1)} custom-call(f32[128,128]{1,0:T(8,128)S(1)} %cholesky.443), custom_call_target="Cholesky" | custom-call | tf_op jit(solution)/shard_map/jit(cholesky)/cholesky | solution.py:30
  768.1 10.0 %custom-call.34 = f32[1,128,128]{1,2,0:T(8,128)S(1)} custom-call(f32[1,128,128]{2,1,0:T(8,128)S(1)} %get-tuple-element.56), custom_call_target="InvertDiagBlocksLowerTriangular" | custom-call | tf_op jit(solution)/shard_map/jit(cholesky)/cholesky | solution.py:30
  780.4 11.7 %cholesky.398 = f32[128,128]{1,0:T(8,128)S(1)} custom-call(f32[128,128]{1,0:T(8,128)S(1)} %cholesky.448), custom_call_target="Cholesky" | custom-call | tf_op jit(solution)/shard_map/jit(cholesky)/cholesky | solution.py:30
  804.8 11.7 %cholesky.415 = f32[128,128]{1,0:T(8,128)S(1)} custom-call(f32[128,128]{1,0:T(8,128)S(1)} %convolution_subtract_fusion.14), custom_call_target="Cholesky" | custom-call | tf_op jit(solution)/shard_map/jit(cholesky)/cholesky | solution.py:30
  824.7 11.2 %while.5 = (s32[]{:T(128)}, f32[512,512]{1,0:T(8,128)}, s32[4,2]{0,1:T(2,128)S(1)}, f32[4,128,128]{2,1,0:T(8,128)S(1)}, s32[]{:T(128)}) while((s32[]{:T(128)}, f32[512,512]{1,0:T(8,128)}, s32[4,2]{0,1:T(2,128)S(1)}, f32[4,128,128]{2,1,0:T(8,128)S(1)}, s32[]{:T(128)}) %tuple.79), condition=%wide.while_cond.clone, body=%wide.while_body.clone.sunk | while | flops 2 | bytes 131189 | solution.py:31
  836.6 40.5 %custom-call.36 = f32[4,128,128]{1,2,0:T(8,128)S(1)} custom-call(f32[4,128,128]{2,1,0:T(8,128)} %copy-done.18), custom_call_target="InvertDiagBlocksLowerTriangular" | custom-call | tf_op jit(solution)/shard_map/jit(_cho_solve)/triangular_solve | solution.py:31
  901.4 16.0 %convolution_subtract_fusion = f32[1024,2048]{1,0:T(8,128)} fusion(f32[1024,2048]{1,0:T(8,128)S(1)} %bitcast.157, f32[512,1024]{1,0:T(8,128)S(1)} %copy-done.4, f32[128,2048]{1,0:T(8,128)S(1)} %fusion.102, f32[128,2048]{1,0:T(8,128)S(1)} %fusion.100, f32[128,2048]{1,0:T(8,128)S(1)} %fusion.98, f32[128,2048]{1,0:T(8,128)S(1)} %fusion.97), kind=kOutput, calls=%fused_computation.7 | convolution fusion | flops 12890144768 | bytes 23068672 | tf_op jit(solution)/shard_map/dot_general | solution.py:54
  (177 shorter events, 172.6 us)
Async XLA Ops:
  7.2 160.2 %copy-start = (f32[1024,440]{0,1:T(8,128)S(1)}, f32[1024,440]{0,1:T(8,128)}, u32[]{:S(2)}) copy-start(f32[1024,440]{0,1:T(8,128)} %param.8) | copy-start | bytes 5406724
  7.2 5.4 copy-start.19
  7.2 160.1 %all-reduce.20.cloned.1.call-start = ((), (), s32[]{:S(2)}) async-start(), calls=%async_computation.5 | async-start | bytes 3604480 | tf_op jit(solution)/shard_map/psum | solution.py:11
  12.6 335.7 %all-reduce.10.cloned.1.call-start = ((), (), s32[]{:S(2)}) async-start(), calls=%async_computation | async-start | bytes 4194304 | tf_op jit(solution)/shard_map/psum | solution.py:43
  178.6 3.8 copy-start.5
  178.6 3.8 copy-start.17
  199.4 263.1 %all-reduce.12.cloned.1.call-start = ((), (), s32[]{:S(2)}) async-start(), calls=%async_computation.1 | async-start | bytes 8388608 | tf_op jit(solution)/shard_map/psum | solution.py:52
  217.5 365.8 %all-reduce.14.cloned.1.call-start = ((), (), s32[]{:S(2)}) async-start(), calls=%async_computation.2 | async-start | bytes 8388608 | tf_op jit(solution)/shard_map/psum | solution.py:52
  358.8 114.0 %copy-start.16 = (f32[512,512]{1,0:T(8,128)S(1)}, f32[512,512]{1,0:T(8,128)}, u32[]{:S(2)}) copy-start(f32[512,512]{1,0:T(8,128)} %copy-done.15) | copy-start | bytes 3145732
  462.6 291.8 %all-reduce.16.cloned.1.call-start = ((), (), s32[]{:S(2)}) async-start(), calls=%async_computation.3 | async-start | bytes 8388608 | tf_op jit(solution)/shard_map/psum | solution.py:52
  543.5 47.9 %copy-start.12 = (f32[512,512]{1,0:T(8,128)}, f32[512,512]{1,0:T(8,128)S(1)}, u32[]{:S(2)}) copy-start(f32[512,512]{1,0:T(8,128)S(1)} %get-tuple-element.185) | copy-start | bytes 3145732
  585.6 3.5 copy-start.13
  595.6 12.3 %slice-start.2 = ((s8[8388608]{0:T(1024)(128)(4,1)}), s8[4194304]{0:T(1024)(128)(4,1)S(1)}, s32[]{:S(2)}) async-start(s8[8388608]{0:T(1024)(128)(4,1)} %bitcast.158), calls=%async_computation.8 | async-start | bytes 8388608
  598.7 7.2 copy-start.8
  601.2 6.7 slice-start.3
  602.3 3.7 copy-start.10
  602.3 5.6 copy-start.7
  607.9 19.5 %copy-start.4 = (f32[512,1024]{1,0:T(8,128)S(1)}, f32[512,1024]{1,0:T(8,128)}, u32[]{:S(2)}) copy-start(f32[512,1024]{1,0:T(8,128)} %copy-done.3) | copy-start | bytes 6291460
  642.7 238.7 %all-reduce.18.cloned.1.call-start = ((), (), s32[]{:S(2)}) async-start(), calls=%async_computation.4 | async-start | bytes 8388608 | tf_op jit(solution)/shard_map/psum | solution.py:52
  883.7 3.5 copy-start.11
  883.7 3.5 copy-start.14
  894.8 6.6 slice-start
  897.3 4.1 slice-start.1
  919.6 4.0 copy-start.1
  (6 other events, 11.0 us)
Sparse Core Ops, SparseCore 0:
  13.6 153.6 all-reduce.19
  199.5 148.6 all-reduce.9
  352.2 110.3 all-reduce.11
  464.8 92.4 all-reduce.13
  642.8 111.5 all-reduce.15
  756.7 92.4 all-reduce.17
